TPU v7x, 32 devices: a whole 2x2x4 slice. The times are simulated.
32 devices in a mesh: hap: 2 (over x), snp: 16 (over z, y, core).
Axes of the slice: x: 2, y: 2, z: 4, core: 2. Of those that a mesh axis runs over, the one named last changes fastest.
Arguments:
- packed_panel: int32 [96, 16384], P('hap', 'snp'), may hold values from 0 to 8191, as said below
- components: bfloat16 [64, 1248], P(None, 'hap'), may hold values from -0.15625 to 0.15625
- bounds: int32 [2, 16384], P(None, 'snp'), may hold values from 0 to 16383, as said below
- band_width: int32 [16384], P('snp'), may hold values from 1 to 256
Outputs:
- ld_scores: float32 [16384], P('snp')
Inputs may be any that keep to these rules, and one draw needn't show every extreme that they name: Bit j of packed_panel[w, s] (j from 0 to 12) is the allele of haplotype 13 w + j at SNP s; higher bits are zero. LD blocks are consecutive runs of 1 to 2048 SNPs that cover all SNPs in order; bounds[0, s] and bounds[1, s] are the first and last SNP of the block holding s.
All inputs are finite; a program needn't handle non-finite values.
Results may differ from a plain program's by a relative error of at most 0.00074.
Values may be sent and summed in bfloat16 or wider, within the bound.
No kernel may reach another device: no remote copies, remote signals or barrier semaphores. Data moves between devices by JAX's collectives and lax.ppermute only.
A program may use at most 64 MiB of HBM per device.

v0:
```python
import jax
import jax.numpy as jnp
from jax import lax
from jax.sharding import PartitionSpec as P

epsilon = 1e-06


def padded_2(block, sides, width):
    for axis, dim in sides:
        count = lax.axis_size(axis)
        forward = [(i, i + 1) for i in range(count - 1)]
        backward = [(target, source) for source, target in forward]
        low = lax.ppermute(
            lax.slice_in_dim(block, block.shape[dim] - width, None, axis=dim), axis, forward
        )
        high = lax.ppermute(lax.slice_in_dim(block, 0, width, axis=dim), axis, backward)
        block = jnp.concatenate([low, block, high], axis=dim)
    return block


def unpack(packed):
    shifts = jnp.arange(13, dtype=jnp.int32)
    bit_values = jnp.bitwise_and(jnp.right_shift(packed[:, None, :], shifts[None, :, None]), 1)
    return bit_values.reshape(packed.shape[0] * 13, packed.shape[1]).astype(jnp.bfloat16)


def project(components, packed_panel):
    column_count = packed_panel.shape[1]
    block_size = min(256, column_count)
    zeroed = jnp.zeros((components.shape[0], column_count), jnp.float32)

    def add_block(block_index, accumulated):
        packed = lax.dynamic_slice_in_dim(packed_panel, block_index * block_size, block_size, 1)
        product = jnp.dot(components, unpack(packed), preferred_element_type=jnp.float32)
        return lax.dynamic_update_slice_in_dim(accumulated, product, block_index * block_size, 1)

    return lax.fori_loop(0, column_count // block_size, add_block, zeroed)


def standardize(factor):
    average = jnp.mean(factor, axis=1, keepdims=True)
    centered = factor - average
    variance = jnp.mean(centered * centered, axis=1, keepdims=True)
    return (centered * lax.rsqrt(variance + epsilon)).astype(jnp.bfloat16)


def band_scores(padded, inverse, bounds, band_width, offset, start_row, row_count, reach_width):
    component_count = padded.shape[0]
    block_size = min(256, row_count)

    def block_scores(block_index):
        first_row = start_row + block_index * block_size
        row_part = lax.dynamic_slice_in_dim(padded, first_row + reach_width, block_size, 1)
        column_part = lax.dynamic_slice_in_dim(padded, first_row, block_size + 2 * reach_width, 1)
        inverse_rows = lax.dynamic_slice_in_dim(inverse, first_row + reach_width, block_size, 0)
        inverse_columns = lax.dynamic_slice_in_dim(
            inverse, first_row, block_size + 2 * reach_width, 0
        )
        block_first = lax.dynamic_slice_in_dim(bounds[0], first_row, block_size, 0)
        block_last = lax.dynamic_slice_in_dim(bounds[1], first_row, block_size, 0)
        row_reach = lax.dynamic_slice_in_dim(band_width, first_row, block_size, 0)
        inner_products = lax.dot_general(
            row_part, column_part, (((0,), (0,)), ((), ())), preferred_element_type=jnp.float32
        )
        correlation = (
            inner_products
            * (1.0 / component_count)
            * inverse_rows[:, None]
            * inverse_columns[None, :]
        )
        row_position = offset + first_row + jnp.arange(block_size, dtype=jnp.int32)
        column_position = (
            offset
            + first_row
            - reach_width
            + jnp.arange(block_size + 2 * reach_width, dtype=jnp.int32)
        )
        window_low = jnp.maximum(block_first, row_position - row_reach)
        window_high = jnp.minimum(block_last, row_position + row_reach)
        inside = (
            (column_position[None, :] >= window_low[:, None])
            & (column_position[None, :] <= window_high[:, None])
            & (column_position[None, :] != row_position[:, None])
        )
        squared_sum = jnp.sum(jnp.where(inside, correlation * correlation, 0.0), axis=1)
        window_count = jnp.sum(inside.astype(jnp.float32), axis=1)
        return component_count * squared_sum / jnp.maximum(window_count, 1.0)

    blocks = jnp.arange(row_count // block_size, dtype=jnp.int32)
    return lax.map(block_scores, blocks).reshape(row_count)


def on_device(packed_panel, components, bounds, band_width):
    partial_factor = project(components, packed_panel)
    column_count = partial_factor.shape[1]
    factor = lax.psum(partial_factor, "hap")
    component_rows = lax.all_to_all(factor, "snp", split_axis=0, concat_axis=1, tiled=True)
    scaled = standardize(component_rows)
    normed = lax.all_to_all(scaled, "snp", split_axis=1, concat_axis=0, tiled=True)
    reach_width = column_count // 4
    padded = padded_2(normed, (("snp", 1),), reach_width)
    inverse = lax.rsqrt(jnp.mean(jnp.square(padded.astype(jnp.float32)), axis=0) + epsilon)
    offset = lax.axis_index("snp") * column_count
    share_rows = column_count // lax.axis_size("hap")
    own_scores = band_scores(
        padded,
        inverse,
        bounds,
        band_width,
        offset,
        lax.axis_index("hap") * share_rows,
        share_rows,
        reach_width,
    )
    return lax.all_gather(own_scores, "hap", axis=0, tiled=True)


def solution(mesh):
    in_specs = (P("hap", "snp"), P(None, "hap"), P(None, "snp"), P("snp"))
    out_specs = P("snp")
    return jax.shard_map(
        on_device, mesh=mesh, in_specs=in_specs, out_specs=out_specs, check_vma=False
    )
```

profile of v0, /device:TPU:13, one launch (start us, length us, event | category | flops | bytes accessed | tf_op | source)
XLA Modules:
  0.0 91.0 jit_solution(2346714453307130350)
XLA Ops:
  6.5 0.0 all-reduce.2.cloned.1.call-start
  6.5 0.0 copy-start
  6.6 0.9 copy-done
  7.4 5.6 %while.25 = (s32[]{:T(128)}, f32[64,1024]{1,0:T(8,128)S(1)}, s32[48,1024]{1,0:T(8,128)}, bf16[64,624]{1,0:T(8,128)(2,1)S(1)}, s32[]{:T(128)}, /*index=5*/s32[]{:T(128)}, s32[]{:T(128)}, s32[]{:T(128)}) while((s32[]{:T(128)}, f32[64,1024]{1,0:T(8,128)S(1)}, s32[48,1024]{1,0:T(8,128)}, bf16[64,624]{1,0:T(8,128)(2,1)S(1)}, s32[]{:T(128)}, ...), condition=%wide.region_1.0_spmd, body=%wide.region_0.0_spmd.sunk | while | flops 20926468 | bytes 2862539 | solution.py:38
  7.4 0.8 constant_dynamic-slice_fusion.6
  8.2 0.1 shift_right_arithmetic.50
  8.3 0.1 shift_right_arithmetic.51
  8.4 0.1 shift_right_arithmetic.53
  8.5 0.3 fusion.22
  8.8 0.8 constant_dynamic-slice_fusion.6
  9.6 0.1 shift_right_arithmetic.50
  9.7 0.1 shift_right_arithmetic.51
  9.8 0.1 shift_right_arithmetic.53
  9.9 0.3 fusion.22
  10.3 0.8 constant_dynamic-slice_fusion.6
  11.1 0.1 shift_right_arithmetic.50
  11.1 0.1 shift_right_arithmetic.51
  11.2 0.1 shift_right_arithmetic.53
  11.4 0.3 fusion.22
  11.7 0.8 constant_dynamic-slice_fusion.6
  12.5 0.1 shift_right_arithmetic.50
  12.5 0.1 shift_right_arithmetic.51
  12.6 0.1 shift_right_arithmetic.53
  12.8 0.3 fusion.22
  13.1 0.8 all_to_all.22
  13.8 0.0 all-reduce.2.cloned.1.call-update
  13.9 24.1 %all-reduce.2.cloned.1.call-done = f32[16,4,1024]{2,1,0:T(4,128)} async-done(((f32[16,4,1024]{2,1,0:T(4,128)}), f32[16,4,1024]{2,1,0:T(4,128)}) %all-reduce.2.cloned.1.call-update) | async-done | bytes 262160 | tf_op jit(solution)/shard_map/psum | solution.py:97
  37.9 14.8 %all_to_all.29 = f32[16,4,1024]{2,1,0:T(4,128)S(1)} all-to-all(f32[16,4,1024]{2,1,0:T(4,128)} %all-reduce.2.cloned.1.call-done), channel_id=1, replica_groups=mesh['hap'=2,'snp'=16] {'snp'}, dimensions={0} | all-to-all | bytes 524288 | tf_op jit(solution)/shard_map/all_to_all | solution.py:98
  52.7 0.3 reduce_sum.51
  53.0 0.3 multiply_reduce_fusion.1
  53.3 0.1 fusion.11
  53.5 9.9 %all_to_all.30 = bf16[4,16,1024]{2,0,1:T(4,128)(2,1)S(1)} all-to-all(bf16[4,16,1024]{2,0,1:T(4,128)(2,1)S(1)} %fusion.11), channel_id=1, replica_groups=mesh['hap'=2,'snp'=16] {'snp'}, dimensions={1} | all-to-all | bytes 262144 | tf_op jit(solution)/shard_map/all_to_all | solution.py:100
  63.4 3.7 %collective-permute-start = (bf16[64,256]{1,0:T(8,128)(2,1)S(1)}, bf16[64,256]{1,0:T(8,128)(2,1)S(1)}, u32[]{:S(2)}, u32[]{:S(2)}) collective-permute-start(bf16[64,256]{1,0:T(8,128)(2,1)S(1)} %get-tuple-element.232), channel_id=1, source_target_pairs={{0,1},{1,2},{2,3},{3,4},{4,5},{5,6},{6,7},{7,8},{8,9},{9,10},{10,1... | collective-permute-start | bytes 98312 | tf_op jit(solution)/shard_map/ppermute | solution.py:14
  67.1 1.9 %collective-permute-start.1 = (bf16[64,256]{1,0:T(8,128)(2,1)S(1)}, bf16[64,256]{1,0:T(8,128)(2,1)S(1)}, u32[]{:S(2)}, u32[]{:S(2)}) collective-permute-start(bf16[64,256]{1,0:T(8,128)(2,1)S(1)} %get-tuple-element.231), channel_id=1, source_target_pairs={{1,0},{2,1},{3,2},{4,3},{5,4},{6,5},{7,6},{8,7},{9,8},{10,9},{11,1... | collective-permute-start | bytes 98312 | tf_op jit(solution)/shard_map/ppermute | solution.py:17
  69.1 0.0 collective-permute-done
  69.1 4.2 %collective-permute-done.1 = bf16[64,256]{1,0:T(8,128)(2,1)S(1)} collective-permute-done((bf16[64,256]{1,0:T(8,128)(2,1)S(1)}, bf16[64,256]{1,0:T(8,128)(2,1)S(1)}, u32[]{:S(2)}, u32[]{:S(2)}) %collective-permute-start.1) | collective-permute-done | bytes 32800 | tf_op jit(solution)/shard_map/ppermute | solution.py:17
  73.3 0.1 multiply_reduce_fusion
  73.3 0.0 copy-start.1
  73.4 0.7 copy-done.1
  74.0 6.3 %while.26 = (s32[]{:T(128)}, f32[2,256]{1,0:T(2,128)S(1)}, s32[2]{0:T(128)S(1)}, s32[]{:T(128)}, s32[]{:T(128)}, /*index=5*/s32[2,1024]{1,0:T(2,128)S(1)}, s32[1...) while((s32[]{:T(128)}, f32[2,256]{1,0:T(2,128)S(1)}, ...), condition=%wide.region_9.10_spmd, body=%wide.region_6.9_spmd.sunk | while | flops 28510736 | bytes 194922 | solution.py:91
  74.0 0.6 dynamic_slice.80
  75.4 0.8 subtract_maximum_fusion.2
  76.1 0.1 dynamic-slice_multiply_fusion.2
  76.2 0.1 dynamic_slice.81
  76.3 0.5 fusion.26
  76.8 0.3 convert_reduce_fusion.2
  77.2 0.6 dynamic_slice.80
  78.5 0.8 subtract_maximum_fusion.2
  79.3 0.1 dynamic-slice_multiply_fusion.2
  79.4 0.1 dynamic_slice.81
  79.5 0.5 fusion.26
  80.0 0.3 convert_reduce_fusion.2
  80.4 3.2 %all-gather = f32[2,1,512]{2,1,0:T(1,128)S(1)} all-gather(f32[1,1,512]{2,1,0:T(1,128)S(1)} %reshape.97), channel_id=1, replica_groups=mesh['hap'=2,'snp'=16] {'hap'}, dimensions={0}, use_global_device_ids=true | all-gather | bytes 6144 | tf_op jit(solution)/shard_map/all_gather | solution.py:116
  83.6 0.6 copy.23
  (28 shorter events, 0.3 us)
Async XLA Ops:
  6.5 31.4 %all-reduce.2.cloned.1.call-start = ((), (), s32[]{:S(2)}) async-start(), calls=%async_computation.2 | async-start | bytes 524288 | tf_op jit(solution)/shard_map/psum | solution.py:97
  6.5 0.9 copy-start
  63.4 5.7 %collective-permute-start = (bf16[64,256]{1,0:T(8,128)(2,1)S(1)}, bf16[64,256]{1,0:T(8,128)(2,1)S(1)}, u32[]{:S(2)}, u32[]{:S(2)}) collective-permute-start(bf16[64,256]{1,0:T(8,128)(2,1)S(1)} %get-tuple-element.232), channel_id=1, source_target_pairs={{0,1},{1,2},{2,3},{3,4},{4,5},{5,6},{6,7},{7,8},{8,9},{9,10},{10,1... | collective-permute-start | bytes 98312 | tf_op jit(solution)/shard_map/ppermute | solution.py:14
  67.1 6.1 %collective-permute-start.1 = (bf16[64,256]{1,0:T(8,128)(2,1)S(1)}, bf16[64,256]{1,0:T(8,128)(2,1)S(1)}, u32[]{:S(2)}, u32[]{:S(2)}) collective-permute-start(bf16[64,256]{1,0:T(8,128)(2,1)S(1)} %get-tuple-element.231), channel_id=1, source_target_pairs={{1,0},{2,1},{3,2},{4,3},{5,4},{6,5},{7,6},{8,7},{9,8},{10,9},{11,1... | collective-permute-start | bytes 98312 | tf_op jit(solution)/shard_map/ppermute | solution.py:17
  73.3 0.7 copy-start.1
Sparse Core Ops, SparseCore 0:
  14.0 23.8 all-reduce.1
where the time goes:
time: 91.7 us; the launch traced here: 91 us
  waiting for transfers between devices  28.2 us (31%)
  blocking collectives  27.9 us (30%)
  between operations  13.5 us (15%)
  local copies, waits for them, and re-layouts  8.78 us (10%)
  starting transfers between devices  5.62 us (6%)
  other arithmetic  3.17 us (3%)
  matrix products  2.22 us (2%)
  loops' own time  1.59 us (2%)
    psum x1, waiting for transfers between devices, on_device(): factor = lax.psum(partial_factor, 'hap')  24.1 us
    all_to_all x1, blocking collectives, on_device(): lax.all_to_all(factor, 'snp', split_axis=0, concat_axis=1, tiled=True)  14.8 us
    all_to_all x1, blocking collectives, on_device(): lax.all_to_all(scaled, 'snp', split_axis=1, concat_axis=0, tiled=True)  9.91 us
    ppermute x1, waiting for transfers between devices, padded_2(): lax.ppermute(lax.slice_in_dim(block, 0, width, axis=dim), axis, backward)  4.16 us
    ppermute x1, starting transfers between devices, padded_2(): lax.ppermute(lax.slice_in_dim(block, block.shape[dim] - width, None, axis...  3.7 us
    dynamic_slice x4, local copies, waits for them, and re-layouts, add_block(): lax.dynamic_slice_in_dim(packed_panel, block_index * block_size, block_si...  3.23 us
    all_gather x1, blocking collectives, on_device(): return lax.all_gather(own_scores, 'hap', axis=0, tiled=True)  3.21 us
    unnamed x8, local copies, waits for them, and re-layouts  2.16 us
  transfers between devices with their start and end apart: 3, of which 2 were waited for; matrix products, arithmetic and copies ran while one was open for 0% of the time, Pallas kernels for 0%

commit v1 on v0

--- a/solution.py
+++ b/solution.py
@@ -94,7 +94,8 @@
 def on_device(packed_panel, components, bounds, band_width):
     partial_factor = project(components, packed_panel)
     column_count = partial_factor.shape[1]
-    factor = lax.psum(partial_factor, "hap")
+    parts = lax.all_gather(partial_factor, "hap", axis=0, tiled=False)
+    factor = parts.sum(axis=0)
     component_rows = lax.all_to_all(factor, "snp", split_axis=0, concat_axis=1, tiled=True)
     scaled = standardize(component_rows)
     normed = lax.all_to_all(scaled, "snp", split_axis=1, concat_axis=0, tiled=True)

time: 91.7 us -> 61.7 us (0.67)
  waiting for transfers between devices: 28.2 us -> 4.17 us
  between operations: 13.5 us -> 0.13 us
  blocking collectives: 27.9 us -> 36.1 us
    psum x1 -> x0, waiting for transfers between devices: 24.1 us -> none  [on_device(): factor = lax.psum(partial_factor, 'hap')]
    all_gather x0 -> x1, blocking collectives: none -> 7.85 us  [on_device(): parts = lax.all_gather(partial_factor, 'hap', axis=0, tiled=False)]
  transfers between devices with their start and end apart: 3 -> 2, of which waited for: 2 -> 1; matrix products, arithmetic and copies ran while one was open for 0% -> 0% of each run, Pallas kernels for 0% -> 0%
where the time goes in v1:
time: 61.7 us; the launch traced here: 61.1 us
  blocking collectives  36.1 us (59%)
  local copies, waits for them, and re-layouts  8.08 us (13%)
  starting transfers between devices  5.62 us (9%)
  waiting for transfers between devices  4.17 us (7%)
  other arithmetic  3.2 us (5%)
  matrix products  2.22 us (4%)
  loops' own time  1.59 us (3%)
    all_to_all x1, blocking collectives, on_device(): lax.all_to_all(factor, 'snp', split_axis=0, concat_axis=1, tiled=True)  15.1 us
    all_to_all x1, blocking collectives, on_device(): lax.all_to_all(scaled, 'snp', split_axis=1, concat_axis=0, tiled=True)  9.91 us
    all_gather x1, blocking collectives, on_device(): parts = lax.all_gather(partial_factor, 'hap', axis=0, tiled=False)  7.85 us
    ppermute x1, waiting for transfers between devices, padded_2(): lax.ppermute(lax.slice_in_dim(block, 0, width, axis=dim), axis, backward)  4.16 us
    ppermute x1, starting transfers between devices, padded_2(): lax.ppermute(lax.slice_in_dim(block, block.shape[dim] - width, None, axis...  3.7 us
    dynamic_slice x4, local copies, waits for them, and re-layouts, add_block(): lax.dynamic_slice_in_dim(packed_panel, block_index * block_size, block_si...  3.23 us
    all_gather x1, blocking collectives, on_device(): return lax.all_gather(own_scores, 'hap', axis=0, tiled=True)  3.21 us
    unnamed x8, local copies, waits for them, and re-layouts  2.16 us
  transfers between devices with their start and end apart: 2, of which 1 were waited for; matrix products, arithmetic and copies ran while one was open for 0% of the time, Pallas kernels for 0%

profile of v1, /device:TPU:13, one launch (start us, length us, event | category | flops | bytes accessed | tf_op | source)
XLA Modules:
  0.0 61.1 jit_solution(8962924693431162730)
XLA Ops:
  0.0 0.0 copy-start
  0.0 0.9 %copy-done = bf16[64,624]{1,0:T(8,128)(2,1)S(1)} copy-done((bf16[64,624]{1,0:T(8,128)(2,1)S(1)}, bf16[64,624]{1,0:T(8,128)(2,1)}, u32[]{:S(2)}) %copy-start) | copy-done | bytes 79896
  0.9 5.6 %while.25 = (s32[]{:T(128)}, f32[64,1024]{1,0:T(8,128)S(1)}, s32[48,1024]{1,0:T(8,128)}, bf16[64,624]{1,0:T(8,128)(2,1)S(1)}, s32[]{:T(128)}, /*index=5*/s32[]{:T(128)}, s32[]{:T(128)}, s32[]{:T(128)}) while((s32[]{:T(128)}, f32[64,1024]{1,0:T(8,128)S(1)}, s32[48,1024]{1,0:T(8,128)}, bf16[64,624]{1,0:T(8,128)(2,1)S(1)}, s32[]{:T(128)}, ...), condition=%wide.region_1.0_spmd, body=%wide.region_0.0_spmd.sunk | while | flops 20926468 | bytes 2862539 | solution.py:38
  0.9 0.8 %constant_dynamic-slice_fusion.6 = s32[48,256]{1,0:T(8,128)S(1)} fusion(s32[48,1024]{1,0:T(8,128)} %get-tuple-element.341, s32[]{:T(128)S(6)} %select_n.45), kind=kLoop, calls=%fused_computation.5.clone.1 | loop fusion | bytes 98308 | tf_op jit(solution)/shard_map/while/body/eval_jaxpr/dynamic_slice | solution.py:34
  1.7 0.1 shift_right_arithmetic.50
  1.8 0.1 shift_right_arithmetic.51
  1.9 0.1 shift_right_arithmetic.53
  2.0 0.3 fusion.22
  2.3 0.8 %constant_dynamic-slice_fusion.6 = s32[48,256]{1,0:T(8,128)S(1)} fusion(s32[48,1024]{1,0:T(8,128)} %get-tuple-element.341, s32[]{:T(128)S(6)} %select_n.45), kind=kLoop, calls=%fused_computation.5.clone.1 | loop fusion | bytes 98308 | tf_op jit(solution)/shard_map/while/body/eval_jaxpr/dynamic_slice | solution.py:34
  3.1 0.1 shift_right_arithmetic.50
  3.2 0.1 shift_right_arithmetic.51
  3.3 0.1 shift_right_arithmetic.53
  3.4 0.3 fusion.22
  3.7 0.8 %constant_dynamic-slice_fusion.6 = s32[48,256]{1,0:T(8,128)S(1)} fusion(s32[48,1024]{1,0:T(8,128)} %get-tuple-element.341, s32[]{:T(128)S(6)} %select_n.45), kind=kLoop, calls=%fused_computation.5.clone.1 | loop fusion | bytes 98308 | tf_op jit(solution)/shard_map/while/body/eval_jaxpr/dynamic_slice | solution.py:34
  4.5 0.1 shift_right_arithmetic.50
  4.6 0.1 shift_right_arithmetic.51
  4.7 0.1 shift_right_arithmetic.53
  4.8 0.3 fusion.22
  5.1 0.8 %constant_dynamic-slice_fusion.6 = s32[48,256]{1,0:T(8,128)S(1)} fusion(s32[48,1024]{1,0:T(8,128)} %get-tuple-element.341, s32[]{:T(128)S(6)} %select_n.45), kind=kLoop, calls=%fused_computation.5.clone.1 | loop fusion | bytes 98308 | tf_op jit(solution)/shard_map/while/body/eval_jaxpr/dynamic_slice | solution.py:34
  5.9 0.1 shift_right_arithmetic.50
  6.0 0.1 shift_right_arithmetic.51
  6.1 0.1 shift_right_arithmetic.53
  6.2 0.3 fusion.22
  6.5 7.8 %all-gather = f32[128,1024]{1,0:T(8,128)S(1)} all-gather(f32[64,1024]{1,0:T(8,128)S(1)} %get-tuple-element.198), channel_id=2, replica_groups=mesh['hap'=2,'snp'=16] {'hap'}, dimensions={0}, use_global_device_ids=true | all-gather | bytes 786432 | tf_op jit(solution)/shard_map/all_gather | solution.py:97
  14.4 0.1 all_to_all.22
  14.5 15.1 %all_to_all.29 = f32[16,4,1024]{2,1,0:T(4,128)S(1)} all-to-all(f32[16,4,1024]{2,1,0:T(4,128)S(1)} %all_to_all.22), channel_id=1, replica_groups=mesh['hap'=2,'snp'=16] {'snp'}, dimensions={0} | all-to-all | bytes 524288 | tf_op jit(solution)/shard_map/all_to_all | solution.py:99
  29.6 0.3 reduce_sum.61
  29.9 0.3 multiply_reduce_fusion.1
  30.2 0.1 fusion.11
  30.4 9.9 %all_to_all.30 = bf16[4,16,1024]{2,0,1:T(4,128)(2,1)S(1)} all-to-all(bf16[4,16,1024]{2,0,1:T(4,128)(2,1)S(1)} %fusion.11), channel_id=1, replica_groups=mesh['hap'=2,'snp'=16] {'snp'}, dimensions={1} | all-to-all | bytes 262144 | tf_op jit(solution)/shard_map/all_to_all | solution.py:101
  40.3 3.7 %collective-permute-start = (bf16[64,256]{1,0:T(8,128)(2,1)S(1)}, bf16[64,256]{1,0:T(8,128)(2,1)S(1)}, u32[]{:S(2)}, u32[]{:S(2)}) collective-permute-start(bf16[64,256]{1,0:T(8,128)(2,1)S(1)} %get-tuple-element.232), channel_id=1, source_target_pairs={{0,1},{1,2},{2,3},{3,4},{4,5},{5,6},{6,7},{7,8},{8,9},{9,10},{10,1... | collective-permute-start | bytes 98312 | tf_op jit(solution)/shard_map/ppermute | solution.py:14
  44.1 1.9 %collective-permute-start.1 = (bf16[64,256]{1,0:T(8,128)(2,1)S(1)}, bf16[64,256]{1,0:T(8,128)(2,1)S(1)}, u32[]{:S(2)}, u32[]{:S(2)}) collective-permute-start(bf16[64,256]{1,0:T(8,128)(2,1)S(1)} %get-tuple-element.231), channel_id=1, source_target_pairs={{1,0},{2,1},{3,2},{4,3},{5,4},{6,5},{7,6},{8,7},{9,8},{10,9},{11,1... | collective-permute-start | bytes 98312 | tf_op jit(solution)/shard_map/ppermute | solution.py:17
  46.0 0.0 collective-permute-done
  46.0 4.2 %collective-permute-done.1 = bf16[64,256]{1,0:T(8,128)(2,1)S(1)} collective-permute-done((bf16[64,256]{1,0:T(8,128)(2,1)S(1)}, bf16[64,256]{1,0:T(8,128)(2,1)S(1)}, u32[]{:S(2)}, u32[]{:S(2)}) %collective-permute-start.1) | collective-permute-done | bytes 32800 | tf_op jit(solution)/shard_map/ppermute | solution.py:17
  50.2 0.1 multiply_reduce_fusion
  50.2 0.0 copy-start.1
  50.3 0.7 %copy-done.1 = s32[2,1024]{1,0:T(2,128)S(1)} copy-done((s32[2,1024]{1,0:T(2,128)S(1)}, s32[2,1024]{1,0:T(2,128)}, u32[]{:S(2)}) %copy-start.1) | copy-done | bytes 8216
  50.9 6.3 %while.26 = (s32[]{:T(128)}, f32[2,256]{1,0:T(2,128)S(1)}, s32[2]{0:T(128)S(1)}, s32[]{:T(128)}, s32[]{:T(128)}, /*index=5*/s32[2,1024]{1,0:T(2,128)S(1)}, s32[1...) while((s32[]{:T(128)}, f32[2,256]{1,0:T(2,128)S(1)}, ...), condition=%wide.region_9.10_spmd, body=%wide.region_6.9_spmd.sunk | while | flops 28510736 | bytes 194922 | solution.py:91
  50.9 0.6 dynamic_slice.80
  52.3 0.8 %subtract_maximum_fusion.2 = (s32[256]{0:T(256)S(1)}, s32[256]{0:T(256)S(1)}, s32[256]{0:T(256)S(1)}) fusion(s32[256]{0:T(256)S(1)} %bitcast.30, s32[1024]{0:T(1024)} %get-tuple-element.387, s32[]{:T(128)S(6)} %select_n.47, s32[]{:T(128)S(6)} %add.171, s32[256]{0:T(256)S(1)} %bitcast.29), kind=kLoop, calls=%fused_computation.20.clone.1 | loop fusion | flops 1280 | bytes 6152 | tf_op jit(solution)/shard_map/while/body/eval_jaxpr/max | solution.py:79
  53.0 0.1 dynamic-slice_multiply_fusion.2
  53.1 0.1 dynamic_slice.81
  53.2 0.5 fusion.26
  53.7 0.3 convert_reduce_fusion.2
  54.1 0.6 %dynamic_slice.80 = s32[1]{0:T(128)} dynamic-slice(s32[2]{0:T(128)S(1)} %get-tuple-element.383, s32[]{:T(128)} %get-tuple-element.364), dynamic_slice_sizes={1} | dynamic-slice | bytes 12 | tf_op jit(solution)/shard_map/while/body/jit(dynamic_index_in_dim)/dynamic_slice | solution.py:91
  55.4 0.8 %subtract_maximum_fusion.2 = (s32[256]{0:T(256)S(1)}, s32[256]{0:T(256)S(1)}, s32[256]{0:T(256)S(1)}) fusion(s32[256]{0:T(256)S(1)} %bitcast.30, s32[1024]{0:T(1024)} %get-tuple-element.387, s32[]{:T(128)S(6)} %select_n.47, s32[]{:T(128)S(6)} %add.171, s32[256]{0:T(256)S(1)} %bitcast.29), kind=kLoop, calls=%fused_computation.20.clone.1 | loop fusion | flops 1280 | bytes 6152 | tf_op jit(solution)/shard_map/while/body/eval_jaxpr/max | solution.py:79
  56.2 0.1 dynamic-slice_multiply_fusion.2
  56.3 0.1 dynamic_slice.81
  56.4 0.5 fusion.26
  56.9 0.3 convert_reduce_fusion.2
  57.3 3.2 %all-gather.1 = f32[2,1,512]{2,1,0:T(1,128)S(1)} all-gather(f32[1,1,512]{2,1,0:T(1,128)S(1)} %reshape.98), channel_id=1, replica_groups=mesh['hap'=2,'snp'=16] {'hap'}, dimensions={0}, use_global_device_ids=true | all-gather | bytes 6144 | tf_op jit(solution)/shard_map/all_gather | solution.py:117
  60.5 0.6 copy.22
  (29 shorter events, 0.3 us)
Async XLA Ops:
  0.0 0.9 %copy-start = (bf16[64,624]{1,0:T(8,128)(2,1)S(1)}, bf16[64,624]{1,0:T(8,128)(2,1)}, u32[]{:S(2)}) copy-start(bf16[64,624]{1,0:T(8,128)(2,1)} %param.9) | copy-start | bytes 239620
  40.3 5.7 %collective-permute-start = (bf16[64,256]{1,0:T(8,128)(2,1)S(1)}, bf16[64,256]{1,0:T(8,128)(2,1)S(1)}, u32[]{:S(2)}, u32[]{:S(2)}) collective-permute-start(bf16[64,256]{1,0:T(8,128)(2,1)S(1)} %get-tuple-element.232), channel_id=1, source_target_pairs={{0,1},{1,2},{2,3},{3,4},{4,5},{5,6},{6,7},{7,8},{8,9},{9,10},{10,1... | collective-permute-start | bytes 98312 | tf_op jit(solution)/shard_map/ppermute | solution.py:14
  44.1 6.1 %collective-permute-start.1 = (bf16[64,256]{1,0:T(8,128)(2,1)S(1)}, bf16[64,256]{1,0:T(8,128)(2,1)S(1)}, u32[]{:S(2)}, u32[]{:S(2)}) collective-permute-start(bf16[64,256]{1,0:T(8,128)(2,1)S(1)} %get-tuple-element.231), channel_id=1, source_target_pairs={{1,0},{2,1},{3,2},{4,3},{5,4},{6,5},{7,6},{8,7},{9,8},{10,9},{11,1... | collective-permute-start | bytes 98312 | tf_op jit(solution)/shard_map/ppermute | solution.py:17
  50.2 0.7 %copy-start.1 = (s32[2,1024]{1,0:T(2,128)S(1)}, s32[2,1024]{1,0:T(2,128)}, u32[]{:S(2)}) copy-start(s32[2,1024]{1,0:T(2,128)} %param.10) | copy-start | bytes 24580
